TPU v7x, 512 devices: a whole 4x8x8 slice. The times are simulated.
512 devices in a mesh: blk: 8 (over z_hi, core), win: 64 (over x, y, z_lo).
Axes of the slice: x: 4, y: 8, z: 8 (z_hi: 4, z_lo: 2; z = z_hi * 2 + z_lo), core: 2. Of those that a mesh axis runs over, the one named last changes fastest.
Arguments:
- frame_tokens: bfloat16 [8, 64, 128, 1024], P('blk', 'win'), may hold values from -21 to 21, as said below
- w_kv: bfloat16 [1024, 2048], replicated, may hold values from -0.1875 to 0.1875
- w_q: bfloat16 [1024, 1024], P('win'), may hold values from -0.1875 to 0.1875
- w_out: bfloat16 [1024, 1024], P('win'), may hold values from -0.1875 to 0.1875
- slot_tokens: int32 [8, 64, 128], P(None, 'win'), may hold values from 0 to 1023, as said below
- counts: int32 [8, 64], P('blk', 'win'), may hold values from 32 to 128, as said below
Outputs:
- projected: bfloat16 [8, 64, 128, 1024], P('blk', 'win')
Inputs may be any that keep to these rules, and one draw needn't show every extreme that they name: `frame_tokens`: shown draw: a normal law truncated at 6. `slot_tokens`: every slot names a token of its own window. For each frame group and window the 128 slots name tokens of exactly 4 frames, 32 from each; no token of a window is named twice. `counts`: slots below the count are live. Each window has a frame group with all 128 slots live.
All inputs are finite; a program needn't handle non-finite values.
Results may differ from a plain program's by a relative error of at most 0.012.
The roundings to bfloat16 on the way count: a program that leaves them out, or rounds other values in their place, can miss the bound.
Values may be sent and summed in bfloat16 or wider, within the bound.
A program may use at most 64 MiB of HBM per device.

v0:
```python
import jax
import jax.numpy as jnp
from jax import lax
from jax.sharding import PartitionSpec as P

HEADS = 16


def add_rows(left_rows, shard_rows):
    return jnp.dot(left_rows, shard_rows, preferred_element_type=jnp.float32)


def absorb(state_now, key_rows, value_rows, query_heads, score_scale):
    row_peak, total_sum, accum_rows = state_now
    win_dev, slot_count, head_count, head_dim = query_heads.shape
    key_heads = key_rows.reshape(win_dev, -1, head_count, head_dim)
    value_heads = value_rows.reshape(win_dev, -1, head_count, head_dim)
    scores = (
        jnp.einsum("jshd,jkhd->jhsk", query_heads, key_heads, preferred_element_type=jnp.float32)
        * score_scale
    )
    new_peak = jnp.maximum(row_peak, jnp.max(scores, axis=-1))
    raw_weights = jnp.exp(scores - new_peak[..., None])
    total_sum = jnp.sum(raw_weights, axis=-1)
    mixed_rows = jnp.einsum(
        "jhsk,jkhd->jshd",
        raw_weights.astype(jnp.bfloat16),
        value_heads,
        preferred_element_type=jnp.float32,
    )
    accum_rows = mixed_rows
    return (new_peak, total_sum, accum_rows)


def local(frame_tokens, w_kv, w_q, w_out, slot_tokens, counts):
    groups = lax.axis_size("blk")
    group_at = lax.axis_index("blk")
    frames_here, win_dev, window_len, model_width = frame_tokens.shape
    slot_count = slot_tokens.shape[2]
    per_owner = slot_count // min(4, groups)
    head_count = HEADS
    head_dim = model_width // head_count
    score_scale = head_dim ** (-0.5)
    frame_rows = frame_tokens[0]
    source_group = slot_tokens // window_len
    is_mine = source_group == group_at
    mine_count = is_mine.astype(jnp.int32)
    rank_of = jnp.cumsum(mine_count, axis=-1) - mine_count
    place_at = jnp.where(is_mine, rank_of, per_owner)
    slot_onehot = (place_at[..., None] == jnp.arange(per_owner, dtype=jnp.int32)).astype(
        jnp.bfloat16
    )
    token_onehot = (
        (slot_tokens - group_at * window_len)[..., None] == jnp.arange(window_len, dtype=jnp.int32)
    ).astype(jnp.bfloat16)
    selector = jnp.einsum(
        "gjsc,gjsu->gjcu", slot_onehot, token_onehot, preferred_element_type=jnp.float32
    ).astype(jnp.bfloat16)
    outgoing = jnp.einsum(
        "gjcu,jud->jgcd", selector, frame_rows, preferred_element_type=jnp.float32
    ).astype(jnp.bfloat16)
    arrived = lax.all_to_all(outgoing, "blk", split_axis=1, concat_axis=1, tiled=True)
    incoming = arrived.reshape(win_dev, groups * per_owner, model_width)
    own_picks = lax.dynamic_index_in_dim(slot_tokens, group_at, 0, keepdims=False)
    own_source = own_picks // window_len
    hit_table = (own_source[..., None] == jnp.arange(groups, dtype=jnp.int32)).astype(jnp.int32)
    before = jnp.cumsum(hit_table, axis=1) - hit_table
    order_in = jnp.sum(before * hit_table, axis=-1)
    spot_at = own_source * per_owner + order_in
    grab_rows = (spot_at[..., None] == jnp.arange(groups * per_owner, dtype=jnp.int32)).astype(
        jnp.bfloat16
    )
    picked_rows = (
        jnp.einsum("jsr,jrd->jsd", grab_rows, incoming, preferred_element_type=jnp.float32)
        .astype(jnp.bfloat16)
        .reshape(-1, model_width)
    )
    query_flat = add_rows(picked_rows, lax.all_gather(w_q, "win", axis=0, tiled=True))
    query_heads = query_flat.astype(jnp.bfloat16).reshape(win_dev, slot_count, head_count, head_dim)
    initial = (
        jnp.full((win_dev, head_count, slot_count), -1e30, jnp.float32),
        jnp.zeros((win_dev, head_count, slot_count), jnp.float32),
        jnp.zeros((win_dev, slot_count, head_count, head_dim), jnp.float32),
    )
    key_value = jnp.einsum(
        "fjpd,de->jfpe",
        lax.all_gather(frame_tokens, "blk", axis=0, tiled=True),
        w_kv,
        preferred_element_type=jnp.float32,
    ).astype(jnp.bfloat16)
    key_value = key_value.reshape(win_dev, -1, 2 * model_width)
    state_end = absorb(
        initial,
        key_value[..., :model_width],
        key_value[..., model_width:],
        query_heads,
        score_scale,
    )
    final_peak, final_total, final_accum = state_end
    attended = (
        (final_accum / jnp.transpose(final_total, (0, 2, 1))[..., None])
        .astype(jnp.bfloat16)
        .reshape(-1, model_width)
    )
    out_sum = add_rows(attended, lax.all_gather(w_out, "win", axis=0, tiled=True))
    live_mask = (jnp.arange(slot_count, dtype=jnp.int32)[None, :] < counts[0][:, None]).astype(
        jnp.float32
    )
    return (
        (out_sum * live_mask.reshape(-1, 1))
        .astype(jnp.bfloat16)
        .reshape(1, win_dev, slot_count, model_width)
    )


def solution(mesh):
    placed = (
        P("blk", "win", None, None),
        P(),
        P("win", None),
        P("win", None),
        P(None, "win", None),
        P("blk", "win"),
    )
    return jax.shard_map(
        local, mesh=mesh, in_specs=placed, out_specs=P("blk", "win", None, None), check_vma=False
    )
```

profile of v0, /device:TPU:8, one launch (start us, length us, event | category | flops | bytes accessed | tf_op | source)
XLA Modules:
  0.0 670.5 jit_solution(2670747314636077683)
XLA Ops:
  6.5 0.7 all-gather.4.cloned.1.call-update
  7.3 0.7 all-gather.6.cloned.1.call-update
  8.0 0.7 fusion.39
  8.7 0.3 reduce_window_sum.23
  9.0 0.7 broadcast_subtract_fusion
  9.7 2.3 fusion.15
  12.0 10.3 %all-to-all-start = ((bf16[1,8,32,1024]{3,2,0,1:T(8,128)(2,1)}), bf16[1,8,32,1024]{3,2,0,1:T(8,128)(2,1)S(1)}, u32[]{:S(2)}, u32[]{:S(2)}) async-start(bf16[1,8,32,1024]{3,2,0,1:T(8,128)(2,1)} %fusion.15), calls=%async_computation | async-start | bytes 1048576 | tf_op jit(solution)/shard_map/all_to_all | solution.py:62
  22.3 0.7 all-gather.8.cloned.1.call-update
  23.0 0.7 and_select_fusion
  23.8 0.2 reduce_window_sum.22
  24.6 0.2 select_reduce_fusion
  24.8 0.7 multiply_add_fusion
  25.5 30.7 %all-gather.4.cloned.1.call-done = bf16[8,1,128,1024]{3,2,1,0:T(8,128)(2,1)} async-done(((bf16[1,1,128,1024]{3,2,1,0:T(8,128)(2,1)}), bf16[8,1,128,1024]{3,2,1,0:T(8,128)(2,1)}) %all-gather.4.cloned.1.call-update) | async-done | bytes 2097168 | tf_op jit(solution)/shard_map/all_gather | solution.py:87
  56.2 7.4 %fusion.8 = bf16[2048,8,128]{0,2,1:T(8,128)(2,1)S(1)} fusion(bf16[1024,2048]{1,0:T(8,128)(2,1)} %param.7, bf16[8,1,128,1024]{3,2,1,0:T(8,128)(2,1)} %all-gather.4.cloned.1.call-done), kind=kOutput, calls=%fused_computation.9 | convolution fusion | flops 4297064448 | bytes 10485760 | tf_op jit(solution)/shard_map/fjpd,de->jfpe/dot_general | solution.py:85
  63.6 1.8 fusion.41
  65.4 2.6 copy.23
  67.9 2.9 copy.30
  70.8 289.0 %all-gather.6.cloned.1.call-done = bf16[1024,1024]{1,0:T(8,128)(2,1)} async-done(((bf16[16,1024]{1,0:T(8,128)(2,1)}), bf16[1024,1024]{1,0:T(8,128)(2,1)}) %all-gather.6.cloned.1.call-update) | async-done | bytes 2097168 | tf_op jit(solution)/shard_map/all_gather | solution.py:78
  359.8 2.2 convolution_convert_fusion.1
  362.2 1.4 multiply_reduce_fusion
  363.6 1.8 fusion
  365.5 2.0 fusion.21
  367.5 293.7 %all-gather.8.cloned.1.call-done = bf16[1024,1024]{1,0:T(8,128)(2,1)} async-done(((bf16[16,1024]{1,0:T(8,128)(2,1)}), bf16[1024,1024]{1,0:T(8,128)(2,1)}) %all-gather.8.cloned.1.call-update) | async-done | bytes 2097168 | tf_op jit(solution)/shard_map/all_gather | solution.py:105
  661.2 2.8 fusion.17
  (11 shorter events, 0.3 us)
Async XLA Ops:
  6.5 49.7 %all-gather.4.cloned.1.call-start = ((), (), s32[]{:S(2)}) async-start(), calls=%async_computation.1 | async-start | bytes 2359296 | tf_op jit(solution)/shard_map/all_gather | solution.py:87
  7.3 352.6 %all-gather.6.cloned.1.call-start = ((), (), s32[]{:S(2)}) async-start(), calls=%async_computation.2 | async-start | bytes 2129920 | tf_op jit(solution)/shard_map/all_gather | solution.py:78
  12.0 58.8 %all-to-all-start = ((bf16[1,8,32,1024]{3,2,0,1:T(8,128)(2,1)}), bf16[1,8,32,1024]{3,2,0,1:T(8,128)(2,1)S(1)}, u32[]{:S(2)}, u32[]{:S(2)}) async-start(bf16[1,8,32,1024]{3,2,0,1:T(8,128)(2,1)} %fusion.15), calls=%async_computation | async-start | bytes 1048576 | tf_op jit(solution)/shard_map/all_to_all | solution.py:62
  22.3 638.9 %all-gather.8.cloned.1.call-start = ((), (), s32[]{:S(2)}) async-start(), calls=%async_computation.3 | async-start | bytes 2129920 | tf_op jit(solution)/shard_map/all_gather | solution.py:105
  363.6 1.8 copy-start
Sparse Core Ops, SparseCore 0:
  9.5 46.6 all-gather.3
  58.3 301.5 all-gather.5
  361.9 299.2 all-gather.7
where the time goes:
time: 671 us; the launch traced here: 670 us
  waiting for transfers between devices  616 us (92%)
  matrix products  18.1 us (3%)
  between operations  13.9 us (2%)
  starting transfers between devices  10.4 us (2%)
  local copies, waits for them, and re-layouts  7.37 us (1%)
    all_gather x1, waiting for transfers between devices, local(): lax.all_gather(w_out, 'win', axis=0, tiled=True)  294 us
    all_gather x1, waiting for transfers between devices, local(): lax.all_gather(w_q, 'win', axis=0, tiled=True)  289 us
    all_gather x1, waiting for transfers between devices, local(): lax.all_gather(frame_tokens, 'blk', axis=0, tiled=True)  30.7 us
  transfers between devices with their start and end apart: 4, of which 3 were waited for; matrix products, arithmetic and copies ran while one was open for 4% of the time, Pallas kernels for 0%

commit v1 on v0

--- a/solution.py
+++ b/solution.py
@@ -33,6 +33,12 @@
 
 
 def local(frame_tokens, w_kv, w_q, w_out, slot_tokens, counts):
+
+    def field_choose(field):
+        return jnp.concatenate(
+            lax.all_to_all(jnp.stack([field] * lax.axis_size("blk"), axis=0), "blk", 0, 0), axis=0
+        )
+
     groups = lax.axis_size("blk")
     group_at = lax.axis_index("blk")
     frames_here, win_dev, window_len, model_width = frame_tokens.shape
@@ -83,10 +89,7 @@
         jnp.zeros((win_dev, slot_count, head_count, head_dim), jnp.float32),
     )
     key_value = jnp.einsum(
-        "fjpd,de->jfpe",
-        lax.all_gather(frame_tokens, "blk", axis=0, tiled=True),
-        w_kv,
-        preferred_element_type=jnp.float32,
+        "fjpd,de->jfpe", field_choose(frame_tokens), w_kv, preferred_element_type=jnp.float32
     ).astype(jnp.bfloat16)
     key_value = key_value.reshape(win_dev, -1, 2 * model_width)
     state_end = absorb(

time: 671 us -> 635 us (0.946)
  waiting for transfers between devices: 616 us -> 577 us
    all_gather x1, waiting for transfers between devices: 289 us -> 216 us  [local(): lax.all_gather(w_q, 'win', axis=0, tiled=True)]
    all_to_all x0 -> x1, waiting for transfers between devices: none -> 55 us  [field_choose(): lax.all_to_all(jnp.stack([field] * lax.axis_size('blk'), axis=0), 'blk',...]
    all_gather x1 -> x0, waiting for transfers between devices: 30.7 us -> none  [local(): lax.all_gather(frame_tokens, 'blk', axis=0, tiled=True)]
    all_to_all x0 -> x1, starting transfers between devices: none -> 10.3 us  [field_choose(): lax.all_to_all(jnp.stack([field] * lax.axis_size('blk'), axis=0), 'blk',...]
    all_to_all x1, starting transfers between devices: 10.3 us -> 3.49 us  [local(): lax.all_to_all(outgoing, 'blk', split_axis=1, concat_axis=1, tiled=True)]
  transfers between devices with their start and end apart: 4 -> 4, of which waited for: 3 -> 4; matrix products, arithmetic and copies ran while one was open for 4% -> 4% of each run, Pallas kernels for 0% -> 0%
where the time goes in v1:
time: 635 us; the launch traced here: 634 us
  waiting for transfers between devices  577 us (91%)
  matrix products  16.7 us (3%)
  between operations  14.2 us (2%)
  starting transfers between devices  13.8 us (2%)
  local copies, waits for them, and re-layouts  9.9 us (2%)
    all_gather x1, waiting for transfers between devices, local(): lax.all_gather(w_out, 'win', axis=0, tiled=True)  300 us
    all_gather x1, waiting for transfers between devices, local(): lax.all_gather(w_q, 'win', axis=0, tiled=True)  216 us
    all_to_all x1, waiting for transfers between devices, field_choose(): lax.all_to_all(jnp.stack([field] * lax.axis_size('blk'), axis=0), 'blk',...  55 us
  transfers between devices with their start and end apart: 4, of which 4 were waited for; matrix products, arithmetic and copies ran while one was open for 4% of the time, Pallas kernels for 0%

profile of v1, /device:TPU:8, one launch (start us, length us, event | category | flops | bytes accessed | tf_op | source)
XLA Modules:
  0.0 634.2 jit_solution(5890383572439869402)
XLA Ops:
  6.5 0.7 all-gather.3.cloned.1.call-update
  7.3 2.5 stack.2
  9.8 10.3 %all-to-all-start = ((bf16[8,1,1,128,1024]{4,3,2,1,0:T(8,128)(2,1)}), bf16[8,1,1,128,1024]{4,3,2,1,0:T(8,128)(2,1)S(1)}, u32[]{:S(2)}, u32[]{:S(2)}) async-start(bf16[8,1,1,128,1024]{4,3,2,1,0:T(8,128)(2,1)} %stack.2), calls=%async_computation | async-start | bytes 4194304 | tf_op jit(solution)/shard_map/all_to_all | solution.py:39
  20.1 0.7 all-gather.5.cloned.1.call-update
  20.9 0.1 fusion.34
  21.0 0.2 reduce_window_sum.22
  21.8 0.2 select_reduce_fusion
  22.0 0.3 reduce_window_sum.23
  22.3 1.4 fusion.15
  23.7 55.0 %all-to-all-done = bf16[8,1,1,128,1024]{4,3,2,1,0:T(8,128)(2,1)S(1)} async-done(((bf16[8,1,1,128,1024]{4,3,2,1,0:T(8,128)(2,1)}), bf16[8,1,1,128,1024]{4,3,2,1,0:T(8,128)(2,1)S(1)}, u32[]{:S(2)}, u32[]{:S(2)}) %all-to-all-start) | async-done | bytes 2097184 | tf_op jit(solution)/shard_map/all_to_all | solution.py:39
  78.7 3.5 all-to-all-start.1
  82.2 6.9 %fusion.8 = bf16[2048,8,128]{0,2,1:T(8,128)(2,1)S(1)} fusion(bf16[1024,2048]{1,0:T(8,128)(2,1)} %param.7, bf16[8,1,1,128,1024]{4,3,2,1,0:T(8,128)(2,1)S(1)} %all-to-all-done), kind=kOutput, calls=%fused_computation.9 | convolution fusion | flops 4297064448 | bytes 10485760 | tf_op jit(solution)/shard_map/fjpd,de->jfpe/dot_general | solution.py:91
  89.1 1.8 fusion.41
  90.9 2.6 copy.21
  93.4 2.9 copy.28
  96.3 4.2 all-to-all-done.1
  100.5 216.3 %all-gather.3.cloned.1.call-done = bf16[1024,1024]{1,0:T(8,128)(2,1)} async-done(((bf16[16,1024]{1,0:T(8,128)(2,1)}), bf16[1024,1024]{1,0:T(8,128)(2,1)}) %all-gather.3.cloned.1.call-update) | async-done | bytes 2097168 | tf_op jit(solution)/shard_map/all_gather | solution.py:84
  316.8 2.2 convolution_convert_fusion.1
  319.0 0.2 copy.27
  319.2 1.4 multiply_reduce_fusion
  320.6 1.8 fusion
  322.4 2.0 fusion.21
  324.4 300.2 %all-gather.5.cloned.1.call-done = bf16[1024,1024]{1,0:T(8,128)(2,1)} async-done(((bf16[16,1024]{1,0:T(8,128)(2,1)}), bf16[1024,1024]{1,0:T(8,128)(2,1)}) %all-gather.5.cloned.1.call-update) | async-done | bytes 2097168 | tf_op jit(solution)/shard_map/all_gather | solution.py:108
  624.6 2.8 fusion.17
  (15 shorter events, 0.1 us)
Async XLA Ops:
  6.5 15.8 %copy-start.1 = (bf16[1,1,128,1024]{3,2,1,0:T(8,128)(2,1)S(1)}, bf16[1,1,128,1024]{3,2,1,0:T(8,128)(2,1)}, u32[]{:S(2)}) copy-start(bf16[1,1,128,1024]{3,2,1,0:T(8,128)(2,1)} %param.6) | copy-start | bytes 786436
  6.5 14.3 %copy-start.2 = (s32[8,1,128]{2,1,0:T(1,128)S(1)}, s32[8,1,128]{2,1,0:T(1,128)}, u32[]{:S(2)}) copy-start(s32[8,1,128]{2,1,0:T(1,128)} %param.10) | copy-start | bytes 12292
  6.5 310.2 %all-gather.3.cloned.1.call-start = ((), (), s32[]{:S(2)}) async-start(), calls=%async_computation.2 | async-start | bytes 2129920 | tf_op jit(solution)/shard_map/all_gather | solution.py:84
  9.8 68.9 %all-to-all-start = ((bf16[8,1,1,128,1024]{4,3,2,1,0:T(8,128)(2,1)}), bf16[8,1,1,128,1024]{4,3,2,1,0:T(8,128)(2,1)S(1)}, u32[]{:S(2)}, u32[]{:S(2)}) async-start(bf16[8,1,1,128,1024]{4,3,2,1,0:T(8,128)(2,1)} %stack.2), calls=%async_computation | async-start | bytes 4194304 | tf_op jit(solution)/shard_map/all_to_all | solution.py:39
  20.1 604.5 %all-gather.5.cloned.1.call-start = ((), (), s32[]{:S(2)}) async-start(), calls=%async_computation.3 | async-start | bytes 2129920 | tf_op jit(solution)/shard_map/all_gather | solution.py:108
  78.7 21.8 %all-to-all-start.1 = ((bf16[1,8,32,1024]{3,2,0,1:T(8,128)(2,1)}), bf16[1,8,32,1024]{3,2,0,1:T(8,128)(2,1)S(1)}, u32[]{:S(2)}, u32[]{:S(2)}) async-start(bf16[1,8,32,1024]{3,2,0,1:T(8,128)(2,1)} %fusion.15), calls=%async_computation.1 | async-start | bytes 1048576 | tf_op jit(solution)/shard_map/all_to_all | solution.py:68
  320.6 1.8 copy-start
Sparse Core Ops, SparseCore 0:
  9.4 307.2 all-gather.2
  318.9 305.6 all-gather.4
